TPU v7x, 32 devices: a whole 2x2x4 slice. The times are simulated.
32 devices in a mesh: parts: 2 (over y), seq: 4 (over z), sub: 4 (over x, core).
Axes of the slice: x: 2, y: 2, z: 4, core: 2. Of those that a mesh axis runs over, the one named last changes fastest.
Arguments:
- q_space: bfloat16 [16, 512, 2048], P(('parts', 'seq'), None, 'sub'), parts along dimension 0, may hold values from -6 to 6
- k_space: bfloat16 [16, 512, 2048], P(('parts', 'seq'), None, 'sub'), parts along dimension 0, may hold values from -6 to 6
- v_space: bfloat16 [16, 512, 2048], P(('parts', 'seq'), None, 'sub'), parts along dimension 0, may hold values from -6 to 6
- q_time: bfloat16 [16, 4, 128, 2048], P('parts', None, 'seq', 'sub'), parts along dimension 0, may hold values from -6 to 6
- k_time: bfloat16 [16, 4, 128, 2048], P('parts', None, 'seq', 'sub'), parts along dimension 0, may hold values from -6 to 6
- out_weight: bfloat16 [2048, 3072], P('sub', 'seq'), may hold values from -0.125 to 0.125
- cotangent: bfloat16 [16, 512, 3072], P(('parts', 'seq'), 'sub'), parts along dimension 0, may hold values from -6 to 6
Outputs:
- dq_space: bfloat16 [16, 512, 2048], P(('parts', 'seq'), None, 'sub'), parts along dimension 0
- dk_space: bfloat16 [16, 512, 2048], P(('parts', 'seq'), None, 'sub'), parts along dimension 0
- dv_space: bfloat16 [16, 512, 2048], P(('parts', 'seq'), None, 'sub'), parts along dimension 0
- d_weight: float32 [4096, 3072], P(('parts', 'sub'), 'seq'), parts along dimension 0
There are 2 independent parts, one for each index of `parts`. A program takes and returns all parts, laid end to end along the dimension named above; an argument that names none is the same for every part. Nothing has to cross between parts.
All inputs are finite; a program needn't handle non-finite values.
Results may differ from a plain program's by a relative error of at most 0.01.
Values may be sent and summed in bfloat16 or wider, within the bound.
No kernel may reach another device: no remote copies, remote signals or barrier semaphores. Data moves between devices by JAX's collectives and lax.ppermute only.
A program may use at most 128 MiB of HBM per device.

v0:
```python
import math
import jax
import jax.numpy as jnp
from jax import lax
from jax.sharding import PartitionSpec as P

HD = 128


def normalize(scores):
    row_top = jnp.max(scores, axis=-1, keepdims=True)
    raised = jnp.exp(scores - row_top)
    return raised / jnp.sum(raised, axis=-1, keepdims=True)


def space_chances(query, keys):
    scores = jnp.einsum("fqhd,fkhd->fhqk", query, keys, preferred_element_type=jnp.float32) * (
        1.0 / math.sqrt(HD)
    )
    return normalize(scores)


def on_device(q_space, k_space, v_space, q_time, k_time, out_weight, cotangent):
    frame_count, patches, columns = q_space.shape
    head_count = columns // HD
    band_count = lax.axis_size("sub")
    seq_count = lax.axis_size("seq")
    all_frames = frame_count * seq_count
    band_len = patches // band_count
    time_len = band_len // seq_count
    split_shape = (frame_count, patches, head_count, HD)
    space_query = q_space.reshape(split_shape)
    space_keys = k_space.reshape(split_shape)
    space_values = v_space.reshape(split_shape)
    chances = space_chances(space_query, space_keys)
    space_out = jnp.einsum(
        "fhqk,fkhd->fqhd",
        chances.astype(jnp.bfloat16),
        space_values,
        preferred_element_type=jnp.float32,
    ).astype(jnp.bfloat16)
    moved = lax.all_to_all(
        space_out.reshape(frame_count, band_count, band_len, columns),
        "seq",
        split_axis=2,
        concat_axis=0,
        tiled=True,
    )
    time_shape = (all_frames, band_count, time_len, head_count, HD)
    time_query = q_time.reshape(time_shape)
    time_keys = k_time.reshape(time_shape)
    time_values = moved.reshape(time_shape)
    time_scores = jnp.einsum(
        "fbphd,gbphd->bphfg", time_query, time_keys, preferred_element_type=jnp.float32
    ) * (1.0 / math.sqrt(HD))
    time_chances = normalize(time_scores).astype(jnp.bfloat16)
    time_out = jnp.einsum(
        "bphfg,gbphd->fbphd", time_chances, time_values, preferred_element_type=jnp.float32
    ).astype(jnp.bfloat16)
    time_out = time_out.reshape(all_frames, band_count, time_len, columns)
    weight_rows = lax.all_gather(out_weight, "seq", axis=1, tiled=True)
    returned = lax.all_to_all(time_out, "seq", split_axis=0, concat_axis=2, tiled=True)
    frame_out = returned.reshape(frame_count, patches, columns)
    segment = lax.all_gather(cotangent, "sub", axis=1, tiled=True)
    weight_sum = jnp.einsum("fnh,fnd->hd", frame_out, segment, preferred_element_type=jnp.float32)
    update = jnp.einsum("fnd,hd->fnh", segment, weight_rows, preferred_element_type=jnp.float32)
    out_grad = update
    weight_sum, out_grad = (weight_sum, out_grad)
    rounded = out_grad.astype(jnp.bfloat16).reshape(frame_count, band_count, band_len, columns)
    time_grad = lax.all_to_all(rounded, "seq", split_axis=2, concat_axis=0, tiled=True)
    d_weight = lax.psum_scatter(
        weight_sum.astype(jnp.bfloat16), "seq", scatter_dimension=1, tiled=True
    ).astype(jnp.float32)
    value_time = jnp.einsum(
        "bphfg,fbphd->gbphd",
        time_chances,
        time_grad.reshape(time_shape),
        preferred_element_type=jnp.float32,
    ).astype(jnp.bfloat16)
    space_grad = lax.all_to_all(
        value_time.reshape(all_frames, band_count, time_len, columns),
        "seq",
        split_axis=0,
        concat_axis=2,
        tiled=True,
    )
    space_grad = space_grad.reshape(split_shape)
    recomputed = space_chances(space_query, space_keys)
    value_grad = jnp.einsum(
        "fhqk,fqhd->fkhd",
        recomputed.astype(jnp.bfloat16),
        space_grad,
        preferred_element_type=jnp.float32,
    ).astype(jnp.bfloat16)
    chance_grad = jnp.einsum(
        "fqhd,fkhd->fhqk", space_grad, space_values, preferred_element_type=jnp.float32
    )
    centre_term = jnp.sum(recomputed * chance_grad, axis=-1, keepdims=True)
    score_grad = (recomputed * (chance_grad - centre_term) * (1.0 / math.sqrt(HD))).astype(
        jnp.bfloat16
    )
    query_grad = jnp.einsum(
        "fhqk,fkhd->fqhd", score_grad, space_keys, preferred_element_type=jnp.float32
    ).astype(jnp.bfloat16)
    keys_grad = jnp.einsum(
        "fhqk,fqhd->fkhd", score_grad, space_query, preferred_element_type=jnp.float32
    ).astype(jnp.bfloat16)
    flat_shape = (frame_count, patches, columns)
    return (
        query_grad.reshape(flat_shape),
        keys_grad.reshape(flat_shape),
        value_grad.reshape(flat_shape),
        d_weight,
    )


def solution(mesh):
    in_specs = (
        P(("parts", "seq"), None, "sub"),
        P(("parts", "seq"), None, "sub"),
        P(("parts", "seq"), None, "sub"),
        P("parts", None, "seq", "sub"),
        P("parts", None, "seq", "sub"),
        P("sub", "seq"),
        P(("parts", "seq"), "sub", None),
    )
    out_specs = (
        P(("parts", "seq"), None, "sub"),
        P(("parts", "seq"), None, "sub"),
        P(("parts", "seq"), None, "sub"),
        P(("parts", "sub"), "seq"),
    )
    return jax.shard_map(
        on_device, mesh=mesh, in_specs=in_specs, out_specs=out_specs, check_vma=False
    )
```

profile of v0, /device:TPU:0, one launch (start us, length us, event | category | flops | bytes accessed | tf_op | source)
XLA Modules:
  0.0 300.6 jit_solution(187689830887894949)
XLA Ops:
  8.7 1.5 copy.121
  10.2 1.9 copy.120
  12.1 5.1 %fusion.79 = (f32[2,4,512]{2,1,0:T(4,128)S(1)}, f32[2,4,512,512]{2,3,1,0:T(8,128)}) fusion(bf16[2,512,4,128]{1,3,2,0:T(8,128)(2,1)S(1)} %bitcast.79, bf16[2,512,4,128]{1,3,2,0:T(8,128)(2,1)S(1)} %bitcast.81), kind=kOutput, calls=%fused_computation.55 | convolution fusion | flops 543162880 | bytes 10502144 | tf_op jit(solution)/shard_map/sub | solution.py:12
  17.1 5.8 %fusion.40 = bf16[2,512,4,128]{3,1,2,0:T(8,128)(2,1)S(1)} fusion(f32[2,4,512,512]{2,3,1,0:T(8,128)} %get-tuple-element.23, f32[2,4,512]{2,1,0:T(4,128)S(1)} %get-tuple-element.22, bf16[2,512,512]{2,1,0:T(8,128)(2,1)S(1)} %copy-done), kind=kOutput, calls=%fused_computation.33 | convolution fusion | flops 541589504 | bytes 10502144 | tf_op jit(solution)/shard_map/fhqk,fkhd->fqhd/dot_general | solution.py:36
  24.2 1.8 copy.104
  26.0 6.5 %all-to-all-start.2 = ((bf16[2,4,128,512]{3,1,0,2:T(4,128)(2,1)}), bf16[2,4,128,512]{3,1,0,2:T(4,128)(2,1)S(1)}, u32[]{:S(2)}, u32[]{:S(2)}) async-start(bf16[2,4,128,512]{3,1,0,2:T(4,128)(2,1)} %copy.104), calls=%async_computation.2 | async-start | bytes 2097152 | tf_op jit(solution)/shard_map/all_to_all | solution.py:42
  33.8 2.1 reshape.70
  36.0 4.8 %fusion.74 = (f32[4,32,4,8]{3,2,1,0:T(4,128)S(1)}, f32[4,32,4,8,8]{3,4,2,1,0:T(8,128)}) fusion(bf16[8,4,32,4,128]{4,3,2,1,0:T(4,128)(2,1)} %reshape.70, bf16[8,4,32,4,128]{4,3,2,1,0:T(4,128)(2,1)S(1)} %reshape.69), kind=kOutput, calls=%fused_computation.54 | convolution fusion | flops 8486919 | bytes 2244608 | tf_op jit(solution)/shard_map/sub | solution.py:12
  40.7 17.3 %all-to-all-done.2 = bf16[2,4,128,512]{3,1,0,2:T(4,128)(2,1)S(1)} async-done(((bf16[2,4,128,512]{3,1,0,2:T(4,128)(2,1)}), bf16[2,4,128,512]{3,1,0,2:T(4,128)(2,1)S(1)}, u32[]{:S(2)}, u32[]{:S(2)}) %all-to-all-start.2) | async-done | bytes 1048608 | tf_op jit(solution)/shard_map/all_to_all | solution.py:42
  58.6 2.6 fusion.39
  62.2 52.4 %all_to_all.60 = bf16[8,4,32,512]{3,2,1,0:T(8,128)(2,1)S(1)} all-to-all(bf16[8,4,32,512]{3,2,1,0:T(8,128)(2,1)S(1)} %reshape.79), channel_id=1, replica_groups=mesh['parts'=2,'seq'=4,'sub'=4] {'seq'}, dimensions={0} | all-to-all | bytes 2097152 | tf_op jit(solution)/shard_map/all_to_all | solution.py:62
  114.8 7.6 %bitcast_convert_fusion = bf16[512,3072]{1,0:T(8,128)(2,1)} fusion(bf16[2,512,512]{2,1,0:T(8,128)(2,1)S(1)} %bitcast.83, bf16[2,512,3072]{2,1,0:T(8,128)(2,1)} %all-gather.3.cloned.1.call-done), kind=kOutput, calls=%fused_computation.9 | convolution fusion | flops 3222798336 | bytes 10485760 | tf_op jit(solution)/shard_map/fnh,fnd->hd/dot_general | solution.py:65
  122.4 18.3 %all-gather.5.cloned.1.call-done = bf16[512,3072]{1,0:T(8,128)(2,1)} async-done(((bf16[512,768]{1,0:T(8,128)(2,1)}), bf16[512,3072]{1,0:T(8,128)(2,1)}) %all-gather.5.cloned.1.call-update) | async-done | bytes 3145744 | tf_op jit(solution)/shard_map/all_gather | solution.py:61
  140.8 7.1 %fusion.35 = bf16[2,512,512]{2,1,0:T(8,128)(2,1)S(1)} fusion(bf16[2,512,3072]{2,1,0:T(8,128)(2,1)} %all-gather.3.cloned.1.call-done, bf16[512,3072]{1,0:T(8,128)(2,1)} %all-gather.5.cloned.1.call-done), kind=kOutput, calls=%fused_computation.30 | convolution fusion | flops 3221749760 | bytes 10485760 | tf_op jit(solution)/shard_map/fnd,hd->fnh/dot_general | solution.py:66
  148.7 57.4 %all_to_all.61 = bf16[2,4,128,512]{3,1,0,2:T(4,128)(2,1)S(1)} all-to-all(bf16[2,4,128,512]{3,1,0,2:T(4,128)(2,1)S(1)} %copy.85), channel_id=1, replica_groups=mesh['parts'=2,'seq'=4,'sub'=4] {'seq'}, dimensions={2} | all-to-all | bytes 2097152 | tf_op jit(solution)/shard_map/all_to_all | solution.py:70
  206.9 2.6 fusion.38
  210.5 36.4 %all_to_all.62 = bf16[8,4,32,512]{3,2,1,0:T(8,128)(2,1)S(1)} all-to-all(bf16[8,4,32,512]{3,2,1,0:T(8,128)(2,1)S(1)} %reshape.71), channel_id=1, replica_groups=mesh['parts'=2,'seq'=4,'sub'=4] {'seq'}, dimensions={0} | all-to-all | bytes 2097152 | tf_op jit(solution)/shard_map/all_to_all | solution.py:80
  247.9 5.9 %fusion.23 = bf16[2,4,128,512]{3,2,1,0:T(8,128)(2,1)} fusion(bf16[2,512,4,128]{1,3,2,0:T(8,128)(2,1)S(1)} %copy.99, f32[2,4,512,512]{2,3,1,0:T(8,128)} %get-tuple-element.23, f32[2,4,512]{2,1,0:T(4,128)S(1)} %get-tuple-element.22), kind=kOutput, calls=%fused_computation.24 | convolution fusion | flops 541589504 | bytes 10502144 | tf_op jit(solution)/shard_map/fhqk,fqhd->fkhd/dot_general | solution.py:89
  253.8 2.4 copy.113
  256.1 4.4 %fusion.44 = f32[2,4,512,512]{2,3,1,0:T(8,128)} fusion(bf16[2,512,4,128]{1,3,2,0:T(8,128)(2,1)S(1)} %copy.99, bf16[2,512,512]{2,1,0:T(8,128)(2,1)S(1)} %copy-done), kind=kOutput, calls=%fused_computation.35 | convolution fusion | flops 536870912 | bytes 10485760 | tf_op jit(solution)/shard_map/fqhd,fkhd->fhqk/dot_general | solution.py:95
  260.6 15.2 %fusion.29 = bf16[2,4,512,128]{2,3,1,0:T(8,128)(2,1)} fusion(bf16[2,512,4,128]{1,3,2,0:T(8,128)(2,1)S(1)} %bitcast.82, f32[2,4,512,512]{2,3,1,0:T(8,128)} %fusion.44, f32[2,4,512,512]{2,3,1,0:T(8,128)} %get-tuple-element.23, f32[2,4,512]{2,1,0:T(4,128)S(1)} %get-tuple-element.22), kind=kOutput, calls=%fused_computation.26 | convolution fusion | flops 552079872 | bytes 18890752 | tf_op jit(solution)/shard_map/fhqk,fkhd->fqhd/dot_general | solution.py:102
  275.8 2.3 copy.111
  278.1 12.3 %fusion.32 = bf16[2,4,512,128]{2,3,1,0:T(8,128)(2,1)S(1)} fusion(bf16[2,512,4,128]{1,3,2,0:T(8,128)(2,1)S(1)} %bitcast.80, f32[2,4,512,512]{2,3,1,0:T(8,128)} %fusion.44, f32[2,4,512,512]{2,3,1,0:T(8,128)} %get-tuple-element.23, f32[2,4,512]{2,1,0:T(4,128)S(1)} %get-tuple-element.22), kind=kOutput, calls=%fused_computation.27 | convolution fusion | flops 552079872 | bytes 18890752 | tf_op jit(solution)/shard_map/fhqk,fqhd->fkhd/dot_general | solution.py:105
  291.7 2.4 convert_element_type.72
  (36 shorter events, 10.7 us)
Async XLA Ops:
  7.2 10.0 %copy-start = (bf16[2,512,512]{2,1,0:T(8,128)(2,1)S(1)}, bf16[2,512,512]{2,1,0:T(8,128)(2,1)}, u32[]{:S(2)}) copy-start(bf16[2,512,512]{2,1,0:T(8,128)(2,1)} %param.9) | copy-start | bytes 3145732
  7.2 107.6 %all-gather.3.cloned.1.call-start = ((), (), s32[]{:S(2)}) async-start(), calls=%async_computation.5 | async-start | bytes 7864320 | tf_op jit(solution)/shard_map/all_gather | solution.py:64
  7.9 132.9 %all-gather.5.cloned.1.call-start = ((), (), s32[]{:S(2)}) async-start(), calls=%async_computation.6 | async-start | bytes 3932160 | tf_op jit(solution)/shard_map/all_gather | solution.py:61
  10.2 7.0 %copy-start.1 = (bf16[2,512,512]{1,2,0:T(8,128)(2,1)}, bf16[2,512,512]{1,2,0:T(8,128)(2,1)S(1)}, u32[]{:S(2)}) copy-start(bf16[2,512,512]{1,2,0:T(8,128)(2,1)S(1)} %copy.121) | copy-start | bytes 3145732
  12.1 10.9 %copy-start.3 = (bf16[2,512,512]{1,2,0:T(8,128)(2,1)}, bf16[2,512,512]{1,2,0:T(8,128)(2,1)S(1)}, u32[]{:S(2)}) copy-start(bf16[2,512,512]{1,2,0:T(8,128)(2,1)S(1)} %copy.120) | copy-start | bytes 3145732
  26.0 32.0 %all-to-all-start.2 = ((bf16[2,4,128,512]{3,1,0,2:T(4,128)(2,1)}), bf16[2,4,128,512]{3,1,0,2:T(4,128)(2,1)S(1)}, u32[]{:S(2)}, u32[]{:S(2)}) async-start(bf16[2,4,128,512]{3,1,0,2:T(4,128)(2,1)} %copy.104), calls=%async_computation.2 | async-start | bytes 2097152 | tf_op jit(solution)/shard_map/all_to_all | solution.py:42
  32.5 259.2 %reduce-scatter.2.cloned.1.call-start = ((), (), s32[]{:S(2)}) async-start(), calls=%async_computation.7 | async-start | bytes 3932160 | tf_op jit(solution)/shard_map/reduce_scatter | solution.py:71
  253.7 6.8 %copy-start.4 = (bf16[2,512,512]{1,2,0:T(8,128)(2,1)S(1)}, bf16[2,512,512]{1,2,0:T(8,128)(2,1)}, u32[]{:S(2)}) copy-start(bf16[2,512,512]{1,2,0:T(8,128)(2,1)} %copy-done.3) | copy-start | bytes 3145732
  260.6 17.5 %copy-start.2 = (bf16[2,512,512]{1,2,0:T(8,128)(2,1)S(1)}, bf16[2,512,512]{1,2,0:T(8,128)(2,1)}, u32[]{:S(2)}) copy-start(bf16[2,512,512]{1,2,0:T(8,128)(2,1)} %copy-done.1) | copy-start | bytes 3145732
Sparse Core Ops, SparseCore 0:
  9.6 49.0 all-gather.2
  60.3 80.4 all-gather.4
  143.1 83.3 reduce-scatter.1
where the time goes:
time: 301 us
  blocking collectives  146 us (49%)
  matrix products  73.3 us (24%)
  waiting for transfers between devices  37 us (12%)
  local copies, waits for them, and re-layouts  21.2 us (7%)
  between operations  14 us (5%)
  starting transfers between devices  6.55 us (2%)
    all_to_all x1, blocking collectives, on_device(): lax.all_to_all(rounded, 'seq', split_axis=2, concat_axis=0, tiled=True)  57.4 us
    all_to_all x1, blocking collectives, on_device(): lax.all_to_all(time_out, 'seq', split_axis=0, concat_axis=2, tiled=True)  52.4 us
    all_to_all x1, blocking collectives, on_device(): lax.all_to_all(value_time.reshape(all_frames, band_count, time_len, colum...  36.4 us
    all_gather x1, waiting for transfers between devices, on_device(): weight_rows = lax.all_gather(out_weight, 'seq', axis=1, tiled=True)  18.3 us
    all_to_all x1, waiting for transfers between devices, on_device(): lax.all_to_all(space_out.reshape(frame_count, band_count, band_len, colum...  17.3 us
    dot_general x1, matrix products, on_device(): jnp.einsum('fhqk,fkhd->fqhd', score_grad, space_keys, preferred_element_t...  15.2 us
    dot_general x1, matrix products, on_device(): jnp.einsum('fhqk,fqhd->fkhd', score_grad, space_query, preferred_element_...  12.3 us
    sub x2, matrix products, normalize(): raised = jnp.exp(scores - row_top)  9.81 us
  transfers between devices with their start and end apart: 4, of which 2 were waited for; matrix products, arithmetic and copies ran while one was open for 31% of the time, Pallas kernels for 0%

commit v1 on v0

--- a/solution.py
+++ b/solution.py
@@ -58,7 +58,14 @@
         "bphfg,gbphd->fbphd", time_chances, time_values, preferred_element_type=jnp.float32
     ).astype(jnp.bfloat16)
     time_out = time_out.reshape(all_frames, band_count, time_len, columns)
-    weight_rows = lax.all_gather(out_weight, "seq", axis=1, tiled=True)
+    ways, here = (lax.axis_size("seq"), lax.axis_index("seq"))
+    weight_rows, reach = (out_weight, 1)
+    while reach < ways:
+        theirs = lax.ppermute(weight_rows, "seq", [(d, d ^ reach) for d in range(ways)])
+        mine_first = jnp.concatenate([weight_rows, theirs], axis=1)
+        theirs_first = jnp.concatenate([theirs, weight_rows], axis=1)
+        weight_rows = jnp.where(here & reach == 0, mine_first, theirs_first)
+        reach = 2 * reach
     returned = lax.all_to_all(time_out, "seq", split_axis=0, concat_axis=2, tiled=True)
     frame_out = returned.reshape(frame_count, patches, columns)
     segment = lax.all_gather(cotangent, "sub", axis=1, tiled=True)

time: 301 us -> 318 us (1.056)
  waiting for transfers between devices: 37 us -> 135 us
  blocking collectives: 146 us -> 51.1 us
  starting transfers between devices: 6.55 us -> 14.9 us
    ppermute x0 -> x2, waiting for transfers between devices: none -> 66.3 us  [on_device(): lax.ppermute(weight_rows, 'seq', [(d, d ^ reach) for d in range(ways)])]
    all_to_all x0 -> x1, waiting for transfers between devices: none -> 52.7 us  [on_device(): lax.all_to_all(time_out, 'seq', split_axis=0, concat_axis=2, tiled=True)]
    all_to_all x1 -> x0, blocking collectives: 52.4 us -> none  [on_device(): lax.all_to_all(time_out, 'seq', split_axis=0, concat_axis=2, tiled=True)]
    all_to_all x1, blocking collectives: 57.4 us -> 24.1 us  [on_device(): lax.all_to_all(rounded, 'seq', split_axis=2, concat_axis=0, tiled=True)]
    all_gather x1 -> x0, waiting for transfers between devices: 18.3 us -> none  [on_device(): weight_rows = lax.all_gather(out_weight, 'seq', axis=1, tiled=True)]
    all_to_all x1, blocking collectives: 36.4 us -> 27 us  [on_device(): lax.all_to_all(value_time.reshape(all_frames, band_count, time_len, colum...]
    ppermute x0 -> x2, starting transfers between devices: none -> 4.47 us  [on_device(): lax.ppermute(weight_rows, 'seq', [(d, d ^ reach) for d in range(ways)])]
    all_to_all x0 -> x1, starting transfers between devices: none -> 3.52 us  [on_device(): lax.all_to_all(time_out, 'seq', split_axis=0, concat_axis=2, tiled=True)]
  transfers between devices with their start and end apart: 4 -> 6, of which waited for: 2 -> 4; matrix products, arithmetic and copies ran while one was open for 31% -> 31% of each run, Pallas kernels for 0% -> 0%
where the time goes in v1:
time: 318 us; the launch traced here: 317 us
  waiting for transfers between devices  135 us (42%)
  matrix products  74.1 us (23%)
  blocking collectives  51.1 us (16%)
  local copies, waits for them, and re-layouts  21.9 us (7%)
  starting transfers between devices  14.9 us (5%)
  between operations  14.3 us (4%)
  other arithmetic  5.42 us (2%)
    ppermute x2, waiting for transfers between devices, on_device(): lax.ppermute(weight_rows, 'seq', [(d, d ^ reach) for d in range(ways)])  66.3 us
    all_to_all x1, waiting for transfers between devices, on_device(): lax.all_to_all(time_out, 'seq', split_axis=0, concat_axis=2, tiled=True)  52.7 us
    all_to_all x1, blocking collectives, on_device(): lax.all_to_all(value_time.reshape(all_frames, band_count, time_len, colum...  27 us
    all_to_all x1, blocking collectives, on_device(): lax.all_to_all(rounded, 'seq', split_axis=2, concat_axis=0, tiled=True)  24.1 us
    all_to_all x1, waiting for transfers between devices, on_device(): lax.all_to_all(space_out.reshape(frame_count, band_count, band_len, colum...  15.5 us
    dot_general x1, matrix products, on_device(): jnp.einsum('fhqk,fkhd->fqhd', score_grad, space_keys, preferred_element_t...  15.2 us
    dot_general x1, matrix products, on_device(): jnp.einsum('fhqk,fqhd->fkhd', score_grad, space_query, preferred_element_...  12.3 us
    sub x2, matrix products, normalize(): raised = jnp.exp(scores - row_top)  9.8 us
  transfers between devices with their start and end apart: 6, of which 4 were waited for; matrix products, arithmetic and copies ran while one was open for 31% of the time, Pallas kernels for 0%

profile of v1, /device:TPU:0, one launch (start us, length us, event | category | flops | bytes accessed | tf_op | source)
XLA Modules:
  0.0 317.0 jit_solution(4404124092463032195)
XLA Ops:
  11.3 5.1 %fusion.87 = (f32[2,4,512]{2,1,0:T(4,128)S(1)}, f32[2,4,512,512]{2,3,1,0:T(8,128)}) fusion(bf16[2,512,4,128]{1,3,2,0:T(8,128)(2,1)S(1)} %bitcast.81, bf16[2,512,4,128]{1,3,2,0:T(8,128)(2,1)S(1)} %bitcast.83), kind=kOutput, calls=%fused_computation.64 | convolution fusion | flops 543162880 | bytes 10502144 | tf_op jit(solution)/shard_map/sub | solution.py:12
  16.4 5.5 %fusion.47 = bf16[2,512,4,128]{3,1,2,0:T(8,128)(2,1)S(1)} fusion(f32[2,4,512,512]{2,3,1,0:T(8,128)} %get-tuple-element.23, f32[2,4,512]{2,1,0:T(4,128)S(1)} %get-tuple-element.22, bf16[2,512,512]{2,1,0:T(8,128)(2,1)S(1)} %copy-done), kind=kOutput, calls=%fused_computation.41 | convolution fusion | flops 541589504 | bytes 10502144 | tf_op jit(solution)/shard_map/fhqk,fkhd->fqhd/dot_general | solution.py:36
  24.9 6.7 %all-to-all-start.2 = ((bf16[2,4,128,512]{3,1,0,2:T(4,128)(2,1)}), bf16[2,4,128,512]{3,1,0,2:T(4,128)(2,1)S(1)}, u32[]{:S(2)}, u32[]{:S(2)}) async-start(bf16[2,4,128,512]{3,1,0,2:T(4,128)(2,1)} %copy.104), calls=%async_computation.2 | async-start | bytes 2097152 | tf_op jit(solution)/shard_map/all_to_all | solution.py:42
  35.0 2.1 reshape.70
  37.1 4.8 %fusion.82 = (f32[4,32,4,8]{3,2,1,0:T(4,128)S(1)}, f32[4,32,4,8,8]{3,4,2,1,0:T(8,128)}) fusion(bf16[8,4,32,4,128]{4,3,2,1,0:T(4,128)(2,1)} %reshape.70, bf16[8,4,32,4,128]{4,3,2,1,0:T(4,128)(2,1)S(1)} %reshape.69), kind=kOutput, calls=%fused_computation.63 | convolution fusion | flops 8486919 | bytes 2244608 | tf_op jit(solution)/shard_map/sub | solution.py:12
  41.8 15.5 %all-to-all-done.2 = bf16[2,4,128,512]{3,1,0,2:T(4,128)(2,1)S(1)} async-done(((bf16[2,4,128,512]{3,1,0,2:T(4,128)(2,1)}), bf16[2,4,128,512]{3,1,0,2:T(4,128)(2,1)S(1)}, u32[]{:S(2)}, u32[]{:S(2)}) %all-to-all-start.2) | async-done | bytes 1048608 | tf_op jit(solution)/shard_map/all_to_all | solution.py:42
  58.0 2.6 fusion.46
  62.5 3.5 %all-to-all-start.3 = ((bf16[8,4,32,512]{3,2,1,0:T(8,128)(2,1)}), bf16[8,4,32,512]{3,2,1,0:T(8,128)(2,1)S(1)}, u32[]{:S(2)}, u32[]{:S(2)}) async-start(bf16[8,4,32,512]{3,2,1,0:T(8,128)(2,1)} %reshape.79), calls=%async_computation.3 | async-start | bytes 2097152 | tf_op jit(solution)/shard_map/all_to_all | solution.py:69
  67.7 3.0 maximum_select_fusion.1
  70.8 2.5 collective-permute-start.1
  73.2 52.7 %all-to-all-done.3 = bf16[8,4,32,512]{3,2,1,0:T(8,128)(2,1)S(1)} async-done(((bf16[8,4,32,512]{3,2,1,0:T(8,128)(2,1)}), bf16[8,4,32,512]{3,2,1,0:T(8,128)(2,1)S(1)}, u32[]{:S(2)}, u32[]{:S(2)}) %all-to-all-start.3) | async-done | bytes 1048608 | tf_op jit(solution)/shard_map/all_to_all | solution.py:69
  126.1 7.6 %bitcast_convert_fusion = bf16[512,3072]{1,0:T(8,128)(2,1)} fusion(bf16[2,512,512]{2,1,0:T(8,128)(2,1)S(1)} %bitcast.85, bf16[2,512,3072]{2,1,0:T(8,128)(2,1)} %all-gather.2.cloned.1.call-done), kind=kOutput, calls=%fused_computation.9 | convolution fusion | flops 3222798336 | bytes 10485760 | tf_op jit(solution)/shard_map/fnh,fnd->hd/dot_general | solution.py:72
  133.8 64.8 %collective-permute-done.1 = bf16[512,1536]{1,0:T(8,128)(2,1)} collective-permute-done((bf16[512,1536]{1,0:T(8,128)(2,1)}, bf16[512,1536]{1,0:T(8,128)(2,1)}, u32[]{:S(2)}, u32[]{:S(2)}) %collective-permute-start.1) | collective-permute-done | bytes 1572896 | tf_op jit(solution)/shard_map/ppermute | solution.py:64
  198.6 8.2 %fusion.42 = bf16[512,2,512]{0,2,1:T(8,128)(2,1)S(1)} fusion(bf16[2,512,3072]{2,1,0:T(8,128)(2,1)} %all-gather.2.cloned.1.call-done, bf16[512,1536]{1,0:T(8,128)(2,1)} %collective-permute-done.1, bf16[512,1536]{1,0:T(8,128)(2,1)} %maximum_select_fusion.1, pred[]{:T(512)S(6)} %eq.6), kind=kOutput, calls=%fused_computation.38 | convolution fusion | flops 3235905536 | bytes 10485761 | tf_op jit(solution)/shard_map/fnd,hd->fnh/dot_general | solution.py:73
  207.6 24.1 %all_to_all.60 = bf16[2,4,128,512]{3,1,0,2:T(4,128)(2,1)S(1)} all-to-all(bf16[2,4,128,512]{3,1,0,2:T(4,128)(2,1)S(1)} %copy.85), channel_id=1, replica_groups=mesh['parts'=2,'seq'=4,'sub'=4] {'seq'}, dimensions={2} | all-to-all | bytes 2097152 | tf_op jit(solution)/shard_map/all_to_all | solution.py:77
  232.3 2.6 fusion.45
  235.9 27.0 %all_to_all.61 = bf16[8,4,32,512]{3,2,1,0:T(8,128)(2,1)S(1)} all-to-all(bf16[8,4,32,512]{3,2,1,0:T(8,128)(2,1)S(1)} %reshape.71), channel_id=1, replica_groups=mesh['parts'=2,'seq'=4,'sub'=4] {'seq'}, dimensions={0} | all-to-all | bytes 2097152 | tf_op jit(solution)/shard_map/all_to_all | solution.py:87
  264.0 5.9 %fusion.30 = bf16[2,4,128,512]{3,2,1,0:T(8,128)(2,1)} fusion(bf16[2,512,4,128]{1,3,2,0:T(8,128)(2,1)S(1)} %copy.99, f32[2,4,512,512]{2,3,1,0:T(8,128)} %get-tuple-element.23, f32[2,4,512]{2,1,0:T(4,128)S(1)} %get-tuple-element.22), kind=kOutput, calls=%fused_computation.32 | convolution fusion | flops 541589504 | bytes 10502144 | tf_op jit(solution)/shard_map/fhqk,fqhd->fkhd/dot_general | solution.py:96
  269.9 2.4 copy.113
  272.2 4.4 %fusion.51 = f32[2,4,512,512]{2,3,1,0:T(8,128)} fusion(bf16[2,512,4,128]{1,3,2,0:T(8,128)(2,1)S(1)} %copy.99, bf16[2,512,512]{2,1,0:T(8,128)(2,1)S(1)} %copy-done), kind=kOutput, calls=%fused_computation.43 | convolution fusion | flops 536870912 | bytes 10485760 | tf_op jit(solution)/shard_map/fqhd,fkhd->fhqk/dot_general | solution.py:102
  276.7 15.2 %fusion.36 = bf16[2,4,512,128]{2,3,1,0:T(8,128)(2,1)} fusion(bf16[2,512,4,128]{1,3,2,0:T(8,128)(2,1)S(1)} %bitcast.84, f32[2,4,512,512]{2,3,1,0:T(8,128)} %fusion.51, f32[2,4,512,512]{2,3,1,0:T(8,128)} %get-tuple-element.23, f32[2,4,512]{2,1,0:T(4,128)S(1)} %get-tuple-element.22), kind=kOutput, calls=%fused_computation.34 | convolution fusion | flops 552079872 | bytes 18890752 | tf_op jit(solution)/shard_map/fhqk,fkhd->fqhd/dot_general | solution.py:109
  291.9 2.3 copy.111
  294.2 12.3 %fusion.39 = bf16[2,4,512,128]{2,3,1,0:T(8,128)(2,1)S(1)} fusion(bf16[2,512,4,128]{1,3,2,0:T(8,128)(2,1)S(1)} %bitcast.82, f32[2,4,512,512]{2,3,1,0:T(8,128)} %fusion.51, f32[2,4,512,512]{2,3,1,0:T(8,128)} %get-tuple-element.23, f32[2,4,512]{2,1,0:T(4,128)S(1)} %get-tuple-element.22), kind=kOutput, calls=%fused_computation.35 | convolution fusion | flops 552079872 | bytes 18890752 | tf_op jit(solution)/shard_map/fhqk,fqhd->fkhd/dot_general | solution.py:112
  307.8 2.4 convert_element_type.76
  (41 shorter events, 19.7 us)
Async XLA Ops:
  7.2 9.2 %copy-start = (bf16[2,512,512]{2,1,0:T(8,128)(2,1)S(1)}, bf16[2,512,512]{2,1,0:T(8,128)(2,1)}, u32[]{:S(2)}) copy-start(bf16[2,512,512]{2,1,0:T(8,128)(2,1)} %param.9) | copy-start | bytes 3145732
  7.2 118.9 %all-gather.2.cloned.1.call-start = ((), (), s32[]{:S(2)}) async-start(), calls=%async_computation.5 | async-start | bytes 7864320 | tf_op jit(solution)/shard_map/all_gather | solution.py:71
  9.4 7.0 %copy-start.1 = (bf16[2,512,512]{1,2,0:T(8,128)(2,1)}, bf16[2,512,512]{1,2,0:T(8,128)(2,1)S(1)}, u32[]{:S(2)}) copy-start(bf16[2,512,512]{1,2,0:T(8,128)(2,1)S(1)} %copy.121) | copy-start | bytes 3145732
  11.3 10.5 %copy-start.3 = (bf16[2,512,512]{1,2,0:T(8,128)(2,1)}, bf16[2,512,512]{1,2,0:T(8,128)(2,1)S(1)}, u32[]{:S(2)}) copy-start(bf16[2,512,512]{1,2,0:T(8,128)(2,1)S(1)} %copy.120) | copy-start | bytes 3145732
  24.9 32.5 %all-to-all-start.2 = ((bf16[2,4,128,512]{3,1,0,2:T(4,128)(2,1)}), bf16[2,4,128,512]{3,1,0,2:T(4,128)(2,1)S(1)}, u32[]{:S(2)}, u32[]{:S(2)}) async-start(bf16[2,4,128,512]{3,1,0,2:T(4,128)(2,1)} %copy.104), calls=%async_computation.2 | async-start | bytes 2097152 | tf_op jit(solution)/shard_map/all_to_all | solution.py:42
  31.6 36.1 %collective-permute-start = (bf16[512,768]{1,0:T(8,128)(2,1)}, bf16[512,768]{1,0:T(8,128)(2,1)}, u32[]{:S(2)}, u32[]{:S(2)}) collective-permute-start(bf16[512,768]{1,0:T(8,128)(2,1)} %param.12), channel_id=1, source_target_pairs={{0,4},{4,0},{8,12},{12,8},{1,5},{5,1},{9,13},{13,9},{2,6},{6,2},{1... | collective-permute-start | bytes 2359304 | tf_op jit(solution)/shard_map/ppermute | solution.py:64
  58.0 9.7 %copy-start.5 = (bf16[512,768]{1,0:T(8,128)(2,1)S(1)}, bf16[512,768]{1,0:T(8,128)(2,1)}, u32[]{:S(2)}) copy-start(bf16[512,768]{1,0:T(8,128)(2,1)} %param.12) | copy-start | bytes 2359300
  62.5 63.5 %all-to-all-start.3 = ((bf16[8,4,32,512]{3,2,1,0:T(8,128)(2,1)}), bf16[8,4,32,512]{3,2,1,0:T(8,128)(2,1)S(1)}, u32[]{:S(2)}, u32[]{:S(2)}) async-start(bf16[8,4,32,512]{3,2,1,0:T(8,128)(2,1)} %reshape.79), calls=%async_computation.3 | async-start | bytes 2097152 | tf_op jit(solution)/shard_map/all_to_all | solution.py:69
  66.0 241.8 %reduce-scatter.2.cloned.1.call-start = ((), (), s32[]{:S(2)}) async-start(), calls=%async_computation.6 | async-start | bytes 3932160 | tf_op jit(solution)/shard_map/reduce_scatter | solution.py:78
  70.8 127.8 %collective-permute-start.1 = (bf16[512,1536]{1,0:T(8,128)(2,1)}, bf16[512,1536]{1,0:T(8,128)(2,1)}, u32[]{:S(2)}, u32[]{:S(2)}) collective-permute-start(bf16[512,1536]{1,0:T(8,128)(2,1)} %maximum_select_fusion.1), channel_id=1, source_target_pairs={{0,8},{4,12},{8,0},{12,4},{1,9},{5,13},{9,1},{13,5},{2,10},{6,14},... | collective-permute-start | bytes 4718600 | tf_op jit(solution)/shard_map/ppermute | solution.py:64
  269.9 6.8 %copy-start.4 = (bf16[2,512,512]{1,2,0:T(8,128)(2,1)S(1)}, bf16[2,512,512]{1,2,0:T(8,128)(2,1)}, u32[]{:S(2)}) copy-start(bf16[2,512,512]{1,2,0:T(8,128)(2,1)} %copy-done.3) | copy-start | bytes 3145732
  276.7 17.5 %copy-start.2 = (bf16[2,512,512]{1,2,0:T(8,128)(2,1)S(1)}, bf16[2,512,512]{1,2,0:T(8,128)(2,1)}, u32[]{:S(2)}) copy-start(bf16[2,512,512]{1,2,0:T(8,128)(2,1)} %copy-done.1) | copy-start | bytes 3145732
Sparse Core Ops, SparseCore 0:
  9.6 49.0 all-gather.1
  133.9 77.7 reduce-scatter.1
